TPU v7x, 32 devices: a whole 2x2x4 slice. The times are simulated.
32 devices in a mesh: group: 2 (over y), ctx: 4 (over z), feat: 2 (over x), ex: 2 (over core).
Axes of the slice: x: 2, y: 2, z: 4, core: 2. Of those that a mesh axis runs over, the one named last changes fastest.
Arguments:
- hidden: bfloat16 [8, 512, 8192], P(('group', 'feat', 'ex'), 'ctx'), parts along dimension 0, may hold values from -6 to 6
- cotangent: bfloat16 [8, 512, 1024], P(('group', 'feat', 'ex'), 'ctx'), parts along dimension 0, may hold values from -6 to 6
- adapter_down_factor: bfloat16 [8192, 16], replicated, may hold values from -0.0625 to 0.0625
- projection: bfloat16 [16384, 8192], P('ctx', 'feat'), may hold values from -6 to 6
- lengths: int32 [8], P(('group', 'feat', 'ex')), parts along dimension 0, may hold values from 128 to 512, as said below
- slot_example_order: int32 [8], P('group'), parts along dimension 0, may hold values from 0 to 3, each once
Outputs:
- features: float32 [8, 8192], P(('group', 'ex'), 'feat'), parts along dimension 0
There are 2 independent parts, one for each index of `group`. A program takes and returns all parts, laid end to end along the dimension named above; an argument that names none is the same for every part. Nothing has to cross between parts.
Inputs may be any that keep to these rules, and one draw needn't show every extreme that they name: `lengths`: some example has exactly 512 valid positions and some exactly one quarter of 512.
All inputs are finite; a program needn't handle non-finite values.
Results may differ from a plain program's by a relative error of at most 0.0042.
Values may be sent and summed in bfloat16 or wider, within the bound.
No kernel may reach another device: no remote copies, remote signals or barrier semaphores. Data moves between devices by JAX's collectives and lax.ppermute only.
A program may use at most 64 MiB of HBM per device.

v0:
```python
import jax
import jax.numpy as jnp
from jax import lax
from jax.sharding import PartitionSpec as P

FEATS = 8192


def per_device(hidden, cotangent, adapter_down_factor, projection, lengths, slot_example_order):
    ctx_count = lax.axis_size("ctx")
    feat_count = lax.axis_size("feat")
    example_groups = lax.axis_size("ex")
    example_count, token_count, model_width = hidden.shape
    down_factor_rows = jnp.dot(
        hidden.reshape(example_count * token_count, model_width),
        adapter_down_factor,
        preferred_element_type=jnp.float32,
    )
    down_factor_rows = down_factor_rows.astype(jnp.bfloat16).reshape(example_count, token_count, -1)
    position = lax.axis_index("ctx") * token_count + lax.iota(jnp.int32, token_count)
    retain_mask = (position[None, :] < lengths[:, None]).astype(jnp.bfloat16)
    down_factor_rows = down_factor_rows * retain_mask[:, :, None]
    partial_value = jnp.einsum(
        "etr,etj->erj", down_factor_rows, cotangent, preferred_element_type=jnp.float32
    )
    partial_value = partial_value.reshape(example_count, -1)
    block_size = partial_value.shape[1] // ctx_count
    summed_all = lax.psum(partial_value, "ctx")
    owned_rows = lax.dynamic_slice_in_dim(
        summed_all, lax.axis_index("ctx") * block_size, block_size, 1
    )
    grad_rows = owned_rows.astype(jnp.bfloat16)
    projected = jnp.dot(
        lax.all_gather(grad_rows, "feat", axis=0, tiled=True),
        projection,
        preferred_element_type=jnp.float32,
    )
    summed = lax.psum(projected, "ctx")
    squares = lax.psum(jnp.sum(summed * summed, axis=1), "feat")
    scaled = summed / jnp.sqrt(squares / FEATS + 1e-06)[:, None]
    everything = lax.all_gather(scaled, "ex", axis=0, tiled=True)
    arranged = jnp.transpose(
        slot_example_order.reshape(feat_count, example_groups, example_count), (1, 0, 2)
    ).reshape(-1)
    own_rows = everything.shape[0] // example_groups
    wanted = lax.axis_index("ex") * own_rows + lax.iota(jnp.int32, own_rows)
    select = (arranged[None, :] == wanted[:, None]).astype(jnp.float32)
    return jnp.dot(
        select, everything, precision=lax.Precision.HIGHEST, preferred_element_type=jnp.float32
    )


def solution(mesh):
    in_specs = (
        P(("group", "feat", "ex"), "ctx", None),
        P(("group", "feat", "ex"), "ctx", None),
        P(),
        P("ctx", "feat"),
        P(("group", "feat", "ex")),
        P("group"),
    )
    out_specs = P(("group", "ex"), "feat")
    return jax.shard_map(
        per_device, mesh=mesh, in_specs=in_specs, out_specs=out_specs, check_vma=False
    )
```

profile of v0, /device:TPU:0, one launch (start us, length us, event | category | flops | bytes accessed | tf_op | source)
XLA Modules:
  0.0 76.8 jit_solution(9681998552901455173)
XLA Ops:
  0.0 0.0 copy-start
  0.8 0.8 %copy-done = bf16[1,128,8192]{2,1,0:T(8,128)(2,1)S(1)} copy-done((bf16[1,128,8192]{2,1,0:T(8,128)(2,1)S(1)}, bf16[1,128,8192]{2,1,0:T(8,128)(2,1)}, u32[]{:S(2)}) %copy-start) | copy-done | bytes 2097176
  1.6 1.9 %convolution_bitcast_fusion = f32[1,1,16,1024]{3,2,1,0:T(8,128)S(1)} fusion(bf16[8192,16]{0,1:T(8,128)(2,1)} %param.8, bf16[1,128,8192]{2,1,0:T(8,128)(2,1)S(1)} %copy-done, bf16[1,128,1024]{2,1,0:T(8,128)(2,1)} %param.7, bf16[128]{0:T(256)(128)(2,1)S(1)} %compare_convert_fusion), kind=kOutput, calls=%fused_computation.2 | convolution fusion | flops 37752832 | bytes 2687232 | tf_op jit(solution)/shard_map/etr,etj->erj/dot_general | solution.py:23
  3.5 0.1 copy.11
  3.6 32.0 %psum.21 = bf16[1,16384]{1,0:T(2,128)(2,1)S(1)} all-reduce(f32[1,16384]{1,0:T(1,128)S(1)} %bitcast.31), channel_id=1, replica_groups=mesh['group'=2,'ctx'=4,'feat'=2,'ex'=2] {'ctx'}, use_global_device_ids=true, to_apply=%region_0.0 | all-reduce | flops 16384 | bytes 98304 | tf_op jit(solution)/shard_map/psum | solution.py:28
  35.6 4.4 %all-gather = bf16[2,1,4096]{2,1,0:T(2,128)(2,1)S(1)} all-gather(bf16[1,1,4096]{2,1,0:T(2,128)(2,1)S(1)} %convert_bitcast_fusion), channel_id=1, replica_groups=mesh['group'=2,'ctx'=4,'feat'=2,'ex'=2] {'feat'}, dimensions={0}, use_global_device_ids=true | all-gather | bytes 24576 | tf_op jit(solution)/shard_map/all_gather | solution.py:34
  40.0 0.0 copy-start.1
  40.0 12.8 %fusion.11 = f32[2,4096]{1,0:T(2,128)S(1)} fusion(bf16[4096,4096]{1,0:T(8,128)(2,1)} %param.9, bf16[2,1,4096]{2,1,0:T(2,128)(2,1)S(1)} %all-gather), kind=kOutput, calls=%fused_computation.8 | convolution fusion | flops 67108864 | bytes 33603584 | tf_op jit(solution)/shard_map/dot_general | solution.py:33
  52.8 15.8 %psum.22 = f32[2,4096]{1,0:T(2,128)S(1)} all-reduce(f32[2,4096]{1,0:T(2,128)S(1)} %fusion.11), channel_id=1, replica_groups=mesh['group'=2,'ctx'=4,'feat'=2,'ex'=2] {'ctx'}, use_global_device_ids=true, to_apply=%region_1.0 | all-reduce | flops 8192 | bytes 65536 | tf_op jit(solution)/shard_map/psum | solution.py:38
  68.6 0.1 multiply_reduce_fusion
  68.7 4.9 %psum.23 = f32[2]{0:T(128)S(1)} all-reduce(f32[2]{0:T(128)S(1)} %multiply_reduce_fusion), channel_id=1, replica_groups=mesh['group'=2,'ctx'=4,'feat'=2,'ex'=2] {'feat'}, use_global_device_ids=true, to_apply=%region_3.0 | all-reduce | flops 2 | bytes 16 | tf_op jit(solution)/shard_map/psum | solution.py:39
  73.7 0.1 divide_bitcast_fusion
  73.8 1.9 %all-gather.1 = f32[2,2,4096]{2,1,0:T(2,128)S(1)} all-gather(f32[1,2,4096]{2,1,0:T(2,128)S(1)} %divide_bitcast_fusion), channel_id=1, replica_groups=mesh['group'=2,'ctx'=4,'feat'=2,'ex'=2] {'ex'}, dimensions={0}, use_global_device_ids=true | all-gather | bytes 98304 | tf_op jit(solution)/shard_map/all_gather | solution.py:41
  75.6 0.1 reshape.45
  75.7 0.0 copy-done.1
  75.7 0.1 reshape.38
  75.8 0.1 copy.9
  75.9 0.1 eq.15
  76.0 0.9 %fusion.15 = f32[2,4096]{1,0:T(2,128)} fusion(f32[4,4096]{1,0:T(4,128)S(1)} %reshape.45, s32[4]{0:T(128)S(1)} %eq.15, s32[2]{0:T(128)S(1)} %iota_add_fusion), kind=kOutput, calls=%fused_computation.14 | convolution fusion | flops 393224 | bytes 98328 | tf_op jit(solution)/shard_map/dot_general | solution.py:48
  (4 shorter events, 0.0 us)
Async XLA Ops:
  0.0 1.6 %copy-start = (bf16[1,128,8192]{2,1,0:T(8,128)(2,1)S(1)}, bf16[1,128,8192]{2,1,0:T(8,128)(2,1)}, u32[]{:S(2)}) copy-start(bf16[1,128,8192]{2,1,0:T(8,128)(2,1)} %param.6) | copy-start | bytes 6291460
  40.0 35.7 %copy-start.1 = (s32[4]{0:T(128)S(1)}, s32[4]{0:T(128)}, u32[]{:S(2)}) copy-start(s32[4]{0:T(128)} %param.11) | copy-start | bytes 52
where the time goes:
time: 77.1 us; the launch traced here: 76.8 us
  blocking collectives  58.9 us (76%)
  matrix products  15.6 us (20%)
  local copies, waits for them, and re-layouts  1.22 us (2%)
  between operations  0.88 us (1%)
    psum x1, blocking collectives, per_device(): summed_all = lax.psum(partial_value, 'ctx')  32 us
    psum x1, blocking collectives, per_device(): summed = lax.psum(projected, 'ctx')  15.8 us
    dot_general x1, matrix products, per_device(): jnp.dot(lax.all_gather(grad_rows, 'feat', axis=0, tiled=True), projection...  12.8 us
    psum x1, blocking collectives, per_device(): squares = lax.psum(jnp.sum(summed * summed, axis=1), 'feat')  4.93 us
    all_gather x1, blocking collectives, per_device(): lax.all_gather(grad_rows, 'feat', axis=0, tiled=True)  4.41 us
    dot_general x1, matrix products, per_device(): jnp.einsum('etr,etj->erj', down_factor_rows, cotangent, preferred_element...  1.87 us
    all_gather x1, blocking collectives, per_device(): everything = lax.all_gather(scaled, 'ex', axis=0, tiled=True)  1.85 us

commit v1 on v0

--- a/solution.py
+++ b/solution.py
@@ -4,6 +4,18 @@
 from jax.sharding import PartitionSpec as P
 
 FEATS = 8192
+
+
+def gather_by_bits(value, axis, dim):
+    ways, here, turn = (lax.axis_size(axis), lax.axis_index(axis), value.shape[dim])
+    line, have = (value, 1)
+    while have < ways:
+        line = jnp.concatenate(
+            [line, lax.ppermute(line, axis, [(d, (d - have) % ways) for d in range(ways)])],
+            axis=dim,
+        )
+        have = 2 * have
+    return jnp.roll(line, here * turn, axis=dim)
 
 
 def per_device(hidden, cotangent, adapter_down_factor, projection, lengths, slot_example_order):
@@ -31,9 +43,7 @@
     )
     grad_rows = owned_rows.astype(jnp.bfloat16)
     projected = jnp.dot(
-        lax.all_gather(grad_rows, "feat", axis=0, tiled=True),
-        projection,
-        preferred_element_type=jnp.float32,
+        gather_by_bits(grad_rows, "feat", 0), projection, preferred_element_type=jnp.float32
     )
     summed = lax.psum(projected, "ctx")
     squares = lax.psum(jnp.sum(summed * summed, axis=1), "feat")

time: 77.1 us -> 76.3 us (0.990)
  blocking collectives: 58.9 us -> 54.5 us
  waiting for transfers between devices: 0 us -> 2.06 us
  starting transfers between devices: 0 us -> 1.55 us
    all_gather x1 -> x0, blocking collectives: 4.41 us -> none  [per_device(): lax.all_gather(grad_rows, 'feat', axis=0, tiled=True)]
    ppermute x0 -> x1, waiting for transfers between devices: none -> 2.06 us  [gather_by_bits(): lax.ppermute(line, axis, [(d, (d - have) % ways) for d in range(ways)])]
    ppermute x0 -> x1, starting transfers between devices: none -> 1.55 us  [gather_by_bits(): lax.ppermute(line, axis, [(d, (d - have) % ways) for d in range(ways)])]
  transfers between devices with their start and end apart: 0 -> 1, of which waited for: 0 -> 1; matrix products, arithmetic and copies ran while one was open for 0% -> 0% of each run, Pallas kernels for 0% -> 0%
where the time goes in v1:
time: 76.3 us; the launch traced here: 76.1 us
  blocking collectives  54.5 us (71%)
  matrix products  15.6 us (20%)
  waiting for transfers between devices  2.06 us (3%)
  starting transfers between devices  1.55 us (2%)
  local copies, waits for them, and re-layouts  1.21 us (2%)
  between operations  0.86 us (1%)
    psum x1, blocking collectives, per_device(): summed_all = lax.psum(partial_value, 'ctx')  32 us
    psum x1, blocking collectives, per_device(): summed = lax.psum(projected, 'ctx')  15.8 us
    dot_general x1, matrix products, per_device(): jnp.dot(gather_by_bits(grad_rows, 'feat', 0), projection, preferred_eleme...  12.8 us
    psum x1, blocking collectives, per_device(): squares = lax.psum(jnp.sum(summed * summed, axis=1), 'feat')  4.91 us
    ppermute x1, waiting for transfers between devices, gather_by_bits(): lax.ppermute(line, axis, [(d, (d - have) % ways) for d in range(ways)])  2.06 us
    dot_general x1, matrix products, per_device(): jnp.einsum('etr,etj->erj', down_factor_rows, cotangent, preferred_element...  1.93 us
    all_gather x1, blocking collectives, per_device(): everything = lax.all_gather(scaled, 'ex', axis=0, tiled=True)  1.85 us
    ppermute x1, starting transfers between devices, gather_by_bits(): lax.ppermute(line, axis, [(d, (d - have) % ways) for d in range(ways)])  1.55 us
  transfers between devices with their start and end apart: 1, of which 1 were waited for; matrix products, arithmetic and copies ran while one was open for 0% of the time, Pallas kernels for 0%

profile of v1, /device:TPU:0, one launch (start us, length us, event | category | flops | bytes accessed | tf_op | source)
XLA Modules:
  0.0 76.1 jit_solution(12623639687400430393)
XLA Ops:
  0.0 0.0 copy-start
  0.0 0.0 copy-start.1
  0.8 0.8 %copy-done = bf16[1,128,8192]{2,1,0:T(8,128)(2,1)S(1)} copy-done((bf16[1,128,8192]{2,1,0:T(8,128)(2,1)S(1)}, bf16[1,128,8192]{2,1,0:T(8,128)(2,1)}, u32[]{:S(2)}) %copy-start) | copy-done | bytes 2097176
  1.6 1.9 %convolution_bitcast_fusion = f32[1,1,16,1024]{3,2,1,0:T(8,128)S(1)} fusion(bf16[8192,16]{0,1:T(8,128)(2,1)} %param.8, bf16[1,128,8192]{2,1,0:T(8,128)(2,1)S(1)} %copy-done, bf16[1,128,1024]{2,1,0:T(8,128)(2,1)} %param.7, bf16[128]{0:T(256)(128)(2,1)S(1)} %compare_convert_fusion), kind=kOutput, calls=%fused_computation.2 | convolution fusion | flops 37752832 | bytes 2687232 | tf_op jit(solution)/shard_map/etr,etj->erj/dot_general | solution.py:35
  3.5 0.1 copy.9
  3.6 32.0 %psum.21 = bf16[1,16384]{1,0:T(2,128)(2,1)S(1)} all-reduce(f32[1,16384]{1,0:T(1,128)S(1)} %bitcast.26), channel_id=1, replica_groups=mesh['group'=2,'ctx'=4,'feat'=2,'ex'=2] {'ctx'}, use_global_device_ids=true, to_apply=%region_0.0 | all-reduce | flops 16384 | bytes 98304 | tf_op jit(solution)/shard_map/psum | solution.py:40
  35.6 1.6 %collective-permute-start = (bf16[1,4096]{1,0:T(2,128)(2,1)S(1)}, bf16[1,4096]{1,0:T(2,128)(2,1)S(1)}, u32[]{:S(2)}, u32[]{:S(2)}) collective-permute-start(bf16[1,4096]{1,0:T(2,128)(2,1)S(1)} %dynamic-slice_convert_fusion), channel_id=1, source_target_pairs={{0,2},{2,0},{1,3},{3,1},{4,6},{6,4},{5,7},{7,5},{8,10},{10,8},{9,1... | collective-permute-start | bytes 24584 | tf_op jit(solution)/shard_map/ppermute | solution.py:14
  37.2 0.0 copy-done.1
  37.2 0.1 reshape.38
  37.3 0.1 copy.8
  37.4 2.1 %collective-permute-done = bf16[1,4096]{1,0:T(2,128)(2,1)S(1)} collective-permute-done((bf16[1,4096]{1,0:T(2,128)(2,1)S(1)}, bf16[1,4096]{1,0:T(2,128)(2,1)S(1)}, u32[]{:S(2)}, u32[]{:S(2)}) %collective-permute-start) | collective-permute-done | bytes 8224 | tf_op jit(solution)/shard_map/ppermute | solution.py:14
  39.4 12.8 %fusion.14 = f32[2,4096]{1,0:T(2,128)S(1)} fusion(bf16[4096,4096]{1,0:T(8,128)(2,1)} %param.9, s32[]{:T(128)S(6)} %select_n.18, bf16[1,4096]{1,0:T(2,128)(2,1)S(1)} %collective-permute-done, bf16[1,4096]{1,0:T(2,128)(2,1)S(1)} %dynamic-slice_convert_fusion), kind=kOutput, calls=%fused_computation.15 | convolution fusion | flops 67174400 | bytes 33603588 | tf_op jit(solution)/shard_map/dot_general | solution.py:45
  52.3 15.8 %psum.22 = f32[2,4096]{1,0:T(2,128)S(1)} all-reduce(f32[2,4096]{1,0:T(2,128)S(1)} %fusion.14), channel_id=1, replica_groups=mesh['group'=2,'ctx'=4,'feat'=2,'ex'=2] {'ctx'}, use_global_device_ids=true, to_apply=%region_1.2 | all-reduce | flops 8192 | bytes 65536 | tf_op jit(solution)/shard_map/psum | solution.py:48
  68.0 0.1 multiply_reduce_fusion
  68.2 0.1 eq.18
  68.3 4.9 %psum.23 = f32[2]{0:T(128)S(1)} all-reduce(f32[2]{0:T(128)S(1)} %multiply_reduce_fusion), channel_id=1, replica_groups=mesh['group'=2,'ctx'=4,'feat'=2,'ex'=2] {'feat'}, use_global_device_ids=true, to_apply=%region_3.4 | all-reduce | flops 2 | bytes 16 | tf_op jit(solution)/shard_map/psum | solution.py:49
  73.2 0.1 divide_bitcast_fusion
  73.3 1.9 %all-gather = f32[2,2,4096]{2,1,0:T(2,128)S(1)} all-gather(f32[1,2,4096]{2,1,0:T(2,128)S(1)} %divide_bitcast_fusion), channel_id=1, replica_groups=mesh['group'=2,'ctx'=4,'feat'=2,'ex'=2] {'ex'}, dimensions={0}, use_global_device_ids=true | all-gather | bytes 98304 | tf_op jit(solution)/shard_map/all_gather | solution.py:51
  75.1 0.1 reshape.43
  75.2 0.9 %fusion.18 = f32[2,4096]{1,0:T(2,128)} fusion(f32[4,4096]{1,0:T(4,128)S(1)} %reshape.43, s32[4]{0:T(128)S(1)} %eq.18, s32[2]{0:T(128)S(1)} %iota_add_fusion), kind=kOutput, calls=%fused_computation.19 | convolution fusion | flops 393224 | bytes 98328 | tf_op jit(solution)/shard_map/dot_general | solution.py:58
  (4 shorter events, 0.0 us)
Async XLA Ops:
  0.0 1.6 %copy-start = (bf16[1,128,8192]{2,1,0:T(8,128)(2,1)S(1)}, bf16[1,128,8192]{2,1,0:T(8,128)(2,1)}, u32[]{:S(2)}) copy-start(bf16[1,128,8192]{2,1,0:T(8,128)(2,1)} %param.6) | copy-start | bytes 6291460
  0.0 37.2 %copy-start.1 = (s32[4]{0:T(128)S(1)}, s32[4]{0:T(128)}, u32[]{:S(2)}) copy-start(s32[4]{0:T(128)} %param.11) | copy-start | bytes 52
  35.6 3.8 %collective-permute-start = (bf16[1,4096]{1,0:T(2,128)(2,1)S(1)}, bf16[1,4096]{1,0:T(2,128)(2,1)S(1)}, u32[]{:S(2)}, u32[]{:S(2)}) collective-permute-start(bf16[1,4096]{1,0:T(2,128)(2,1)S(1)} %dynamic-slice_convert_fusion), channel_id=1, source_target_pairs={{0,2},{2,0},{1,3},{3,1},{4,6},{6,4},{5,7},{7,5},{8,10},{10,8},{9,1... | collective-permute-start | bytes 24584 | tf_op jit(solution)/shard_map/ppermute | solution.py:14
